TPU v7x, 256 devices: a whole 4x4x8 slice. The times are simulated.
256 devices in a mesh: seq: 16 (over z, x_lo), head: 4 (over x_hi, core), req: 4 (over y).
Axes of the slice: x: 4 (x_hi: 2, x_lo: 2; x = x_hi * 2 + x_lo), y: 4, z: 8, core: 2. Of those that a mesh axis runs over, the one named last changes fastest.
Arguments:
- queries: bfloat16 [32768, 2560], P(('req', 'seq'), 'head'), parts along dimension 0, may hold values from -8 to 8
- keys: bfloat16 [32768, 2560], P(('req', 'seq'), 'head'), parts along dimension 0, may hold values from -8 to 8
- values: bfloat16 [32768, 2560], P(('req', 'seq'), 'head'), parts along dimension 0, may hold values from -8 to 8
- clip_ids: int32 [32768], P('req'), parts along dimension 0, may hold values from 0 to 3, never falling along the last dimension, each value on 1 to 3072 neighbouring positions
- plan: int32 [256], P('req'), parts along dimension 0, may hold values from 0 to 15, as said below
Outputs:
- attended: bfloat16 [32768, 2560], P(('req', 'seq'), 'head'), parts along dimension 0
- log_normalizer: float32 [20, 32768], P('head', ('req', 'seq')), parts along dimension 1
There are 4 independent parts, one for each index of `req`. A program takes and returns all parts, laid end to end along the dimension named above; each array names one. Nothing has to cross between parts.
Inputs may be any that keep to these rules, and one draw needn't show every extreme that they name: `plan`: every index along seq computes exactly 4 blocks, and of the 4 blocks held by one index of seq (blocks k * 4 to k * 4 + 3 on index k) at most 1 go to the same index; some pair of indices reaches 1. `clip_ids`: clip ids never fall along the tokens; each clip holds 1 to 3072 tokens and one holds exactly 3072.
All inputs are finite; a program needn't handle non-finite values.
Results may differ from a plain program's by a relative error of at most 0.007.
Values may be sent and summed in bfloat16 or wider, within the bound.
A program may use at most 128 MiB of HBM per device.

v0:
```python
import jax
import jax.numpy as jnp
from jax import lax
from jax.sharding import PartitionSpec as P

HD = 128
BLOCK = 128


def shards(queries, keys, values, clip_ids, plan):
    group_size = lax.axis_size("seq")
    rank_here = lax.axis_index("seq")
    tok_dev, width_dev = queries.shape
    blocks_dev = tok_dev // BLOCK
    blocks_all = plan.shape[0]
    capacity = (blocks_dev + group_size - 1) // group_size
    slot_count = group_size * capacity
    heads_dev = width_dev // HD
    score_scale = 1.0 / HD**0.5
    block_index = jnp.arange(blocks_all, dtype=jnp.int32)
    source = block_index // blocks_dev
    earlier = (
        (plan[None, :] == plan[:, None])
        & (source[None, :] == source[:, None])
        & (block_index[None, :] < block_index[:, None])
    )
    pair_rank = jnp.sum(earlier, axis=1)
    send_slot = plan * capacity + pair_rank
    recv_slot_all = source * capacity + pair_rank
    local_send = lax.dynamic_slice_in_dim(send_slot, rank_here * blocks_dev, blocks_dev)
    slot_range = jnp.arange(slot_count, dtype=jnp.int32)
    local_range = jnp.arange(blocks_dev, dtype=jnp.int32)
    send_match = slot_range[:, None] == local_send[None, :]
    send_pick = jnp.sum(send_match * local_range[None, :], axis=1)
    send_filled = jnp.any(send_match, axis=1)
    owned_here = plan == rank_here
    position = jnp.cumsum(owned_here.astype(jnp.int32)) - 1
    choose = (local_range[:, None] == position[None, :]) & owned_here[None, :]
    recv_pick = jnp.sum(choose * recv_slot_all[None, :], axis=1)
    back_match = slot_range[:, None] == recv_pick[None, :]
    back_pick = jnp.sum(back_match * local_range[None, :], axis=1)
    back_filled = jnp.any(back_match, axis=1)
    sort_key = plan * blocks_all + block_index
    packed_place = jnp.sum(sort_key[None, :] < sort_key[:, None], axis=1)
    packed_block = jnp.sum(
        (packed_place[None, :] == block_index[:, None]) * block_index[None, :], axis=1
    )
    packed_ids = jnp.take(clip_ids.reshape(blocks_all, BLOCK), packed_block, axis=0).reshape(-1)

    def pack_slots(tokens_dev, picked, filled):
        columns = tokens_dev.shape[1]
        blocked = jnp.take(tokens_dev.reshape(blocks_dev, BLOCK, columns), picked, axis=0)
        blocked = jnp.where(filled[:, None, None], blocked, jnp.zeros_like(blocked))
        return blocked.reshape(group_size, capacity, BLOCK, columns)

    def read_slots(arrived, picked):
        columns = arrived.shape[-1]
        blocked = jnp.take(arrived.reshape(slot_count, BLOCK, columns), picked, axis=0)
        return blocked.reshape(blocks_dev * BLOCK, columns)

    arrived = (
        lax.all_to_all(
            pack_slots(queries, send_pick, send_filled),
            "seq",
            split_axis=0,
            concat_axis=0,
            tiled=True,
        ),
        lax.all_to_all(
            pack_slots(keys, send_pick, send_filled), "seq", split_axis=0, concat_axis=0, tiled=True
        ),
        lax.all_to_all(
            pack_slots(values, send_pick, send_filled),
            "seq",
            split_axis=0,
            concat_axis=0,
            tiled=True,
        ),
    )
    query_rows = read_slots(arrived[0], recv_pick)
    loop_source = (read_slots(arrived[1], recv_pick), read_slots(arrived[2], recv_pick))
    query_ids = lax.dynamic_slice_in_dim(packed_ids, rank_here * tok_dev, tok_dev)
    query_heads = query_rows.reshape(tok_dev, heads_dev, HD)

    def attend_block(state, key_part, value_part, part_ids):
        running_max, running_sum, accumulated = state
        rows = key_part.shape[0]
        scores = (
            jnp.einsum(
                "qhd,khd->hqk",
                query_heads,
                key_part.reshape(rows, heads_dev, HD),
                preferred_element_type=jnp.float32,
            )
            * score_scale
        )
        same_clip = (query_ids[:, None] == part_ids[None, :])[None, :, :]
        masked = jnp.where(same_clip, scores, jnp.float32(-1e30))
        new_max = jnp.maximum(running_max, jnp.max(masked, axis=2))
        weights = jnp.where(same_clip, jnp.exp(masked - new_max[:, :, None]), jnp.float32(0.0))
        rescale = jnp.exp(running_max - new_max)
        running_sum = running_sum * rescale + jnp.sum(weights, axis=2)
        product = jnp.einsum(
            "hqk,khd->qhd",
            weights.astype(jnp.bfloat16),
            value_part.reshape(rows, heads_dev, HD),
            preferred_element_type=jnp.float32,
        )
        accumulated = accumulated * jnp.transpose(rescale)[:, :, None] + product
        return (new_max, running_sum, accumulated)

    start_state = (
        jnp.full((heads_dev, tok_dev), -1e30, jnp.float32),
        jnp.zeros((heads_dev, tok_dev), jnp.float32),
        jnp.zeros((tok_dev, heads_dev, HD), jnp.float32),
    )
    key_part = lax.all_gather(loop_source[0], "seq", axis=0, tiled=True)
    value_part = lax.all_gather(loop_source[1], "seq", axis=0, tiled=True)
    part_ids = packed_ids
    rows = key_part.shape[0]
    sub_count = rows // 512

    def scan_step(inner_state, inputs):
        return (attend_block(inner_state, inputs[0], inputs[1], inputs[2]), None)

    inputs = (
        key_part.reshape(sub_count, 512, width_dev),
        value_part.reshape(sub_count, 512, width_dev),
        part_ids.reshape(sub_count, 512),
    )
    final_state, unused = lax.scan(scan_step, start_state, inputs)
    running_max, running_sum, accumulated = final_state
    finished = (
        (accumulated / jnp.transpose(running_sum)[:, :, None])
        .astype(jnp.bfloat16)
        .reshape(tok_dev, width_dev)
    )
    log_totals = running_max + jnp.log(running_sum)
    returned = lax.all_to_all(
        pack_slots(finished, back_pick, back_filled), "seq", split_axis=0, concat_axis=0, tiled=True
    )
    attended = read_slots(returned, local_send)
    return (attended, log_totals)


def solution(mesh):
    return jax.shard_map(
        shards,
        mesh=mesh,
        in_specs=(
            P(("req", "seq"), "head"),
            P(("req", "seq"), "head"),
            P(("req", "seq"), "head"),
            P("req"),
            P("req"),
        ),
        out_specs=(P(("req", "seq"), "head"), P("head", ("req", "seq"))),
        check_vma=False,
    )
```

profile of v0, /device:TPU:4, one launch (start us, length us, event | category | flops | bytes accessed | tf_op | source)
XLA Modules:
  0.0 998.7 jit_solution(18444506933324885968)
XLA Ops:
  10.0 2.4 gather_fusion.3
  12.4 2.4 gather_fusion.5
  14.8 2.4 gather_fusion.1
  17.1 4.2 fusion.18
  21.4 71.3 %all_to_all.20 = bf16[16,1,128,640]{3,2,1,0:T(8,128)(2,1)} all-to-all(bf16[16,1,128,640]{3,2,1,0:T(8,128)(2,1)S(1)} %get-tuple-element.152), channel_id=1, replica_groups=mesh['seq'=16,'head'=4,'req'=4] {'seq'}, dimensions={0} | all-to-all | bytes 5242880 | tf_op jit(solution)/shard_map/all_to_all | solution.py:69
  92.7 65.1 %all_to_all.21 = bf16[16,1,128,640]{3,2,1,0:T(8,128)(2,1)} all-to-all(bf16[16,1,128,640]{3,2,1,0:T(8,128)(2,1)S(1)} %get-tuple-element.151), channel_id=1, replica_groups=mesh['seq'=16,'head'=4,'req'=4] {'seq'}, dimensions={0} | all-to-all | bytes 5242880 | tf_op jit(solution)/shard_map/all_to_all | solution.py:62
  157.8 3.9 all-to-all-start.2
  162.2 3.3 gather_fusion.2
  165.5 3.2 gather_fusion.4
  168.7 53.8 %all-to-all-done.2 = bf16[16,1,128,640]{3,2,1,0:T(8,128)(2,1)S(1)} async-done(((bf16[16,1,128,640]{3,2,1,0:T(8,128)(2,1)}), bf16[16,1,128,640]{3,2,1,0:T(8,128)(2,1)S(1)}, u32[]{:S(2)}, u32[]{:S(2)}) %all-to-all-start.2) | async-done | bytes 2621472 | tf_op jit(solution)/shard_map/all_to_all | solution.py:72
  222.5 1.5 gather_fusion.6
  224.0 2.8 broadcast_select_fusion.1
  232.9 216.5 %all-gather.3.cloned.1.call-done = bf16[8192,640]{1,0:T(8,128)(2,1)} async-done(((bf16[512,640]{1,0:T(8,128)(2,1)}), bf16[8192,640]{1,0:T(8,128)(2,1)}) %all-gather.3.cloned.1.call-update) | async-done | bytes 10485776 | tf_op jit(solution)/shard_map/all_gather | solution.py:117
  449.4 227.8 %all-gather.5.cloned.1.call-done = bf16[8192,640]{1,0:T(8,128)(2,1)} async-done(((bf16[512,640]{1,0:T(8,128)(2,1)}), bf16[8192,640]{1,0:T(8,128)(2,1)}) %all-gather.5.cloned.1.call-update) | async-done | bytes 10485776 | tf_op jit(solution)/shard_map/all_gather | solution.py:118
  677.2 236.1 %while.15 = (s32[]{:T(128)}, f32[5,512]{1,0:T(8,128)S(1)}, f32[5,512]{1,0:T(8,128)}, f32[512,5,128]{0,2,1:T(8,128)}, s32[512]{0:T(512)}, /*index=5*/s32[16,512]{...) while((s32[]{:T(128)}, f32[5,512]{1,0:T(8,128)S(1)}, ...), condition=%wide.region_11.14_spmd.clone, body=%wide.region_8.0_spmd.clone.sunk | while | flops 689388544 | bytes 42590440 | solution.py:131
  678.9 1.4 constant_dynamic-slice_fusion.6
  680.5 3.5 fusion.43
  684.3 5.4 fusion.47
  693.2 1.4 constant_dynamic-slice_fusion.6
  694.9 3.5 fusion.43
  698.7 5.8 fusion.47
  708.0 1.4 constant_dynamic-slice_fusion.6
  709.7 3.5 fusion.43
  713.5 5.8 fusion.47
  722.8 1.4 constant_dynamic-slice_fusion.6
  724.5 3.5 fusion.43
  728.3 5.8 fusion.47
  737.6 1.4 constant_dynamic-slice_fusion.6
  739.2 3.5 fusion.43
  743.0 5.8 fusion.47
  752.4 1.4 constant_dynamic-slice_fusion.6
  754.0 3.5 fusion.43
  757.8 5.8 fusion.47
  768.8 3.5 fusion.43
  772.6 5.8 fusion.47
  781.9 1.4 constant_dynamic-slice_fusion.6
  783.6 3.5 fusion.43
  787.4 5.8 fusion.47
  798.4 3.5 fusion.43
  802.1 5.8 fusion.47
  811.5 1.4 constant_dynamic-slice_fusion.6
  813.1 3.5 fusion.43
  816.9 5.8 fusion.47
  826.3 1.4 constant_dynamic-slice_fusion.6
  827.9 3.5 fusion.43
  831.7 5.8 fusion.47
  842.7 3.5 fusion.43
  846.5 5.8 fusion.47
  855.8 1.4 constant_dynamic-slice_fusion.6
  857.5 3.5 fusion.43
  861.3 5.8 fusion.47
  872.3 3.5 fusion.43
  876.0 5.8 fusion.47
  887.0 3.5 fusion.43
  890.8 5.8 fusion.47
  900.2 1.4 constant_dynamic-slice_fusion.6
  901.8 3.5 fusion.43
  905.6 5.8 fusion.47
  913.3 1.5 divide_convert_fusion
  917.0 1.9 fusion.17
  919.0 7.6 all-to-all-start.3
  927.2 61.1 %all-to-all-done.3 = bf16[16,1,128,640]{3,2,1,0:T(8,128)(2,1)S(1)} async-done(((bf16[16,1,128,640]{3,2,1,0:T(8,128)(2,1)}), bf16[16,1,128,640]{3,2,1,0:T(8,128)(2,1)S(1)}, u32[]{:S(2)}, u32[]{:S(2)}) %all-to-all-start.3) | async-done | bytes 2621472 | tf_op jit(solution)/shard_map/all_to_all | solution.py:139
  988.4 1.5 gather_fusion.8
  989.8 2.1 broadcast_select_fusion
  (353 shorter events, 83.4 us)
Async XLA Ops:
  7.2 2.8 copy-start
  10.0 2.4 copy-start.2
  12.4 2.4 copy-start.3
  14.8 2.4 copy-start.4
  157.8 3.9 copy-start.9
  157.8 64.7 %all-to-all-start.2 = ((bf16[16,1,128,640]{3,2,1,0:T(8,128)(2,1)}), bf16[16,1,128,640]{3,2,1,0:T(8,128)(2,1)S(1)}, u32[]{:S(2)}, u32[]{:S(2)}) async-start(bf16[16,1,128,640]{3,2,1,0:T(8,128)(2,1)} %get-tuple-element.150), calls=%async_computation.2 | async-start | bytes 5242880 | tf_op jit(solution)/shard_map/all_to_all | solution.py:72
  161.7 287.7 %all-gather.3.cloned.1.call-start = ((), (), s32[]{:S(2)}) async-start(), calls=%async_computation.4 | async-start | bytes 11141120 | tf_op jit(solution)/shard_map/all_gather | solution.py:117
  224.0 4.1 copy-start.5
  226.8 450.4 %all-gather.5.cloned.1.call-start = ((), (), s32[]{:S(2)}) async-start(), calls=%async_computation.5 | async-start | bytes 11141120 | tf_op jit(solution)/shard_map/all_gather | solution.py:118
  684.0 5.7 slice-start
  684.3 5.4 slice-start.1
  689.7 1.3 copy-start.6
  698.4 6.1 slice-start
  698.7 5.8 slice-start.1
  704.5 1.3 copy-start.6
  713.2 6.1 slice-start
  713.5 5.8 slice-start.1
  719.3 1.3 copy-start.6
  728.0 6.1 slice-start
  728.2 5.8 slice-start.1
  734.0 1.3 copy-start.6
  742.7 6.1 slice-start
  743.0 5.8 slice-start.1
  748.8 1.3 copy-start.6
  757.5 6.1 slice-start
  757.8 5.8 slice-start.1
  763.6 1.3 copy-start.6
  772.3 6.1 slice-start
  772.6 5.8 slice-start.1
  778.4 1.3 copy-start.6
  787.1 6.1 slice-start
  787.4 5.8 slice-start.1
  793.1 1.3 copy-start.6
  801.9 6.1 slice-start
  802.1 5.8 slice-start.1
  807.9 1.3 copy-start.6
  816.6 6.1 slice-start
  816.9 5.8 slice-start.1
  822.7 1.3 copy-start.6
  831.4 6.1 slice-start
  831.7 5.8 slice-start.1
  837.5 1.3 copy-start.6
  846.2 6.1 slice-start
  846.5 5.8 slice-start.1
  852.3 1.3 copy-start.6
  861.0 6.1 slice-start
  861.3 5.8 slice-start.1
  867.0 1.3 copy-start.6
  875.8 6.1 slice-start
  876.0 5.8 slice-start.1
  881.8 1.3 copy-start.6
  890.5 6.1 slice-start
  890.8 5.8 slice-start.1
  896.6 1.3 copy-start.6
  905.3 6.1 slice-start
  905.6 5.8 slice-start.1
  911.4 1.3 copy-start.6
  915.8 1.2 copy-start.11
  915.9 1.2 copy-start.12
  919.0 7.6 copy-start.14
  919.0 7.6 copy-start.8
  919.0 70.8 %copy-start.10 = (pred[4]{0:T(512)(128)(4,1)S(1)}, pred[4]{0:T(512)(128)(4,1)}, u32[]{:S(2)}) copy-start(pred[4]{0:T(512)(128)(4,1)} %get-tuple-element.142) | copy-start | bytes 16
  919.0 69.4 %all-to-all-start.3 = ((bf16[16,1,128,640]{3,2,1,0:T(8,128)(2,1)}), bf16[16,1,128,640]{3,2,1,0:T(8,128)(2,1)S(1)}, u32[]{:S(2)}, u32[]{:S(2)}) async-start(bf16[16,1,128,640]{3,2,1,0:T(8,128)(2,1)} %fusion.17), calls=%async_computation.3 | async-start | bytes 5242880 | tf_op jit(solution)/shard_map/all_to_all | solution.py:139
  926.6 65.3 %copy-start.1 = (bf16[512,640]{1,0:T(8,128)(2,1)S(1)}, bf16[512,640]{1,0:T(8,128)(2,1)}, u32[]{:S(2)}) copy-start(bf16[512,640]{1,0:T(8,128)(2,1)} %param.11) | copy-start | bytes 1966084
  (17 other events, 10.3 us)
Sparse Core Ops, SparseCore 0:
  227.0 222.3 all-gather.2
  451.8 225.4 all-gather.4
where the time goes:
time: 1000 us; the launch traced here: 999 us
  waiting for transfers between devices  560 us (56%)
  matrix products  148 us (15%)
  blocking collectives  136 us (14%)
  local copies, waits for them, and re-layouts  73.1 us (7%)
  other arithmetic  54 us (5%)
  between operations  14.3 us (1%)
  starting transfers between devices  11.5 us (1%)
    all_gather x1, waiting for transfers between devices, shards(): value_part = lax.all_gather(loop_source[1], 'seq', axis=0, tiled=True)  228 us
    all_gather x1, waiting for transfers between devices, shards(): key_part = lax.all_gather(loop_source[0], 'seq', axis=0, tiled=True)  217 us
    dot_general x16, matrix products, attend_block(): jnp.einsum('hqk,khd->qhd', weights.astype(jnp.bfloat16), value_part.resha...  92 us
    all_to_all x1, blocking collectives, shards(): lax.all_to_all(pack_slots(keys, send_pick, send_filled), 'seq', split_axi...  71.3 us
    all_to_all x1, blocking collectives, shards(): lax.all_to_all(pack_slots(queries, send_pick, send_filled), 'seq', split_...  65.1 us
    all_to_all x1, waiting for transfers between devices, shards(): lax.all_to_all(pack_slots(finished, back_pick, back_filled), 'seq', split...  61.1 us
    dot_general x16, matrix products, attend_block(): jnp.einsum('qhd,khd->hqk', query_heads, key_part.reshape(rows, heads_dev,...  55.7 us
    all_to_all x1, waiting for transfers between devices, shards(): lax.all_to_all(pack_slots(values, send_pick, send_filled), 'seq', split_a...  53.8 us
  transfers between devices with their start and end apart: 4, of which 4 were waited for; matrix products, arithmetic and copies ran while one was open for 1% of the time, Pallas kernels for 0%

commit v1 on v0

--- a/solution.py
+++ b/solution.py
@@ -115,7 +115,9 @@
         jnp.zeros((tok_dev, heads_dev, HD), jnp.float32),
     )
     key_part = lax.all_gather(loop_source[0], "seq", axis=0, tiled=True)
-    value_part = lax.all_gather(loop_source[1], "seq", axis=0, tiled=True)
+    value_part = jnp.concatenate(
+        lax.all_to_all(jnp.stack([loop_source[1]] * lax.axis_size("seq")), "seq", 0, 0), axis=0
+    )
     part_ids = packed_ids
     rows = key_part.shape[0]
     sub_count = rows // 512

time: 1000 us -> 917 us (0.917)
  waiting for transfers between devices: 560 us -> 499 us
  matrix products: 148 us -> 128 us
  other arithmetic: 54 us -> 40 us
    all_to_all x0 -> x1, waiting for transfers between devices: none -> 284 us  [shards(): lax.all_to_all(jnp.stack([loop_source[1]] * lax.axis_size('seq')), 'seq',...]
    all_gather x1 -> x0, waiting for transfers between devices: 228 us -> none  [shards(): value_part = lax.all_gather(loop_source[1], 'seq', axis=0, tiled=True)]
    all_gather x1, waiting for transfers between devices: 217 us -> 101 us  [shards(): key_part = lax.all_gather(loop_source[0], 'seq', axis=0, tiled=True)]
    dot_general x16, matrix products: 92 us -> 72.3 us  [attend_block(): jnp.einsum('hqk,khd->qhd', weights.astype(jnp.bfloat16), value_part.resha...]
    eq x16, other arithmetic: 14.3 us -> 3.42 us  [attend_block(): same_clip = (query_ids[:, None] == part_ids[None, :])[None, :, :]]
where the time goes in v1:
time: 917 us; the launch traced here: 908 us
  waiting for transfers between devices  499 us (54%)
  blocking collectives  136 us (15%)
  matrix products  128 us (14%)
  local copies, waits for them, and re-layouts  69.1 us (8%)
  other arithmetic  40 us (4%)
  starting transfers between devices  18.2 us (2%)
  between operations  14.3 us (2%)
    all_to_all x1, waiting for transfers between devices, shards(): lax.all_to_all(jnp.stack([loop_source[1]] * lax.axis_size('seq')), 'seq',...  284 us
    all_gather x1, waiting for transfers between devices, shards(): key_part = lax.all_gather(loop_source[0], 'seq', axis=0, tiled=True)  101 us
    dot_general x16, matrix products, attend_block(): jnp.einsum('hqk,khd->qhd', weights.astype(jnp.bfloat16), value_part.resha...  72.3 us
    all_to_all x1, blocking collectives, shards(): lax.all_to_all(pack_slots(keys, send_pick, send_filled), 'seq', split_axi...  71.3 us
    all_to_all x1, blocking collectives, shards(): lax.all_to_all(pack_slots(queries, send_pick, send_filled), 'seq', split_...  65.1 us
    all_to_all x1, waiting for transfers between devices, shards(): lax.all_to_all(pack_slots(finished, back_pick, back_filled), 'seq', split...  60 us
    dot_general x16, matrix products, attend_block(): jnp.einsum('qhd,khd->hqk', query_heads, key_part.reshape(rows, heads_dev,...  55.7 us
    all_to_all x1, waiting for transfers between devices, shards(): lax.all_to_all(pack_slots(values, send_pick, send_filled), 'seq', split_a...  53.9 us
  transfers between devices with their start and end apart: 4, of which 4 were waited for; matrix products, arithmetic and copies ran while one was open for 1% of the time, Pallas kernels for 0%

profile of v1, /device:TPU:4, one launch (start us, length us, event | category | flops | bytes accessed | tf_op | source)
XLA Modules:
  0.0 907.9 jit_solution(11370876937812873643)
XLA Ops:
  9.2 2.4 gather_fusion.3
  11.5 2.4 gather_fusion.5
  13.9 2.4 gather_fusion.1
  16.3 4.2 fusion.18
  20.5 71.3 %all_to_all.25 = bf16[16,1,128,640]{3,2,1,0:T(8,128)(2,1)} all-to-all(bf16[16,1,128,640]{3,2,1,0:T(8,128)(2,1)S(1)} %get-tuple-element.150), channel_id=1, replica_groups=mesh['seq'=16,'head'=4,'req'=4] {'seq'}, dimensions={0} | all-to-all | bytes 5242880 | tf_op jit(solution)/shard_map/all_to_all | solution.py:69
  91.9 65.1 %all_to_all.26 = bf16[16,1,128,640]{3,2,1,0:T(8,128)(2,1)} all-to-all(bf16[16,1,128,640]{3,2,1,0:T(8,128)(2,1)S(1)} %get-tuple-element.149), channel_id=1, replica_groups=mesh['seq'=16,'head'=4,'req'=4] {'seq'}, dimensions={0} | all-to-all | bytes 5242880 | tf_op jit(solution)/shard_map/all_to_all | solution.py:62
  157.0 3.9 all-to-all-start.2
  161.3 3.2 gather_fusion.2
  164.6 3.2 gather_fusion.4
  167.8 53.9 %all-to-all-done.2 = bf16[16,1,128,640]{3,2,1,0:T(8,128)(2,1)S(1)} async-done(((bf16[16,1,128,640]{3,2,1,0:T(8,128)(2,1)}), bf16[16,1,128,640]{3,2,1,0:T(8,128)(2,1)S(1)}, u32[]{:S(2)}, u32[]{:S(2)}) %all-to-all-start.2) | async-done | bytes 2621472 | tf_op jit(solution)/shard_map/all_to_all | solution.py:72
  221.7 1.5 gather_fusion.6
  223.2 2.6 broadcast_select_fusion.1
  226.0 5.0 stack.3
  231.0 5.0 all-to-all-start.3
  239.2 284.0 %all-to-all-done.3 = bf16[16,512,640]{1,2,0:T(8,128)(2,1)} async-done(((bf16[16,512,640]{1,2,0:T(8,128)(2,1)}), bf16[16,512,640]{1,2,0:T(8,128)(2,1)}, u32[]{:S(2)}, u32[]{:S(2)}) %all-to-all-start.3) | async-done | bytes 10485792 | tf_op jit(solution)/shard_map/all_to_all | solution.py:119
  523.1 101.0 %all-gather.2.cloned.1.call-done = bf16[8192,640]{1,0:T(8,128)(2,1)} async-done(((bf16[512,640]{1,0:T(8,128)(2,1)}), bf16[8192,640]{1,0:T(8,128)(2,1)}) %all-gather.2.cloned.1.call-update) | async-done | bytes 10485776 | tf_op jit(solution)/shard_map/all_gather | solution.py:117
  624.1 198.0 %while.15 = (s32[]{:T(128)}, f32[5,512]{1,0:T(8,128)S(1)}, f32[5,512]{1,0:T(8,128)S(1)}, f32[512,5,128]{0,2,1:T(8,128)}, s32[512]{0:T(512)S(1)}, /*index=5*/s32[...) while((s32[]{:T(128)}, f32[5,512]{1,0:T(8,128)S(1)}, ...), condition=%wide.region_11.14_spmd.clone, body=%wide.region_8.0_spmd.clone.sunk | while | flops 689388544 | bytes 51683564 | solution.py:133
  625.8 3.5 fusion.43
  629.3 1.3 constant_dynamic-slice_fusion.8
  630.6 4.5 fusion.47
  638.1 3.5 fusion.43
  641.7 1.3 constant_dynamic-slice_fusion.8
  643.0 4.5 fusion.47
  650.5 3.5 fusion.43
  654.0 1.3 constant_dynamic-slice_fusion.8
  655.3 4.5 fusion.47
  662.9 3.5 fusion.43
  666.4 1.3 constant_dynamic-slice_fusion.8
  667.7 4.5 fusion.47
  675.3 3.5 fusion.43
  678.8 1.3 constant_dynamic-slice_fusion.8
  680.1 4.5 fusion.47
  687.7 3.5 fusion.43
  691.2 1.3 constant_dynamic-slice_fusion.8
  692.5 4.5 fusion.47
  700.0 3.5 fusion.43
  703.5 1.3 constant_dynamic-slice_fusion.8
  704.9 4.5 fusion.47
  712.4 3.5 fusion.43
  715.9 1.3 constant_dynamic-slice_fusion.8
  717.2 4.5 fusion.47
  724.8 3.5 fusion.43
  729.6 4.5 fusion.47
  737.2 3.5 fusion.43
  740.7 1.3 constant_dynamic-slice_fusion.8
  742.0 4.5 fusion.47
  749.6 3.5 fusion.43
  754.4 4.5 fusion.47
  761.9 3.5 fusion.43
  766.8 4.5 fusion.47
  774.3 3.5 fusion.43
  779.1 4.5 fusion.47
  786.7 3.5 fusion.43
  791.5 4.5 fusion.47
  799.1 3.5 fusion.43
  803.9 4.5 fusion.47
  811.5 3.5 fusion.43
  816.3 4.5 fusion.47
  822.2 1.5 divide_convert_fusion
  825.7 1.9 fusion.17
  827.7 9.2 %all-to-all-start.4 = ((bf16[16,1,128,640]{3,2,1,0:T(8,128)(2,1)}), bf16[16,1,128,640]{3,2,1,0:T(8,128)(2,1)S(1)}, u32[]{:S(2)}, u32[]{:S(2)}) async-start(bf16[16,1,128,640]{3,2,1,0:T(8,128)(2,1)} %fusion.17), calls=%async_computation.4 | async-start | bytes 5242880 | tf_op jit(solution)/shard_map/all_to_all | solution.py:141
  837.5 60.0 %all-to-all-done.4 = bf16[16,1,128,640]{3,2,1,0:T(8,128)(2,1)S(1)} async-done(((bf16[16,1,128,640]{3,2,1,0:T(8,128)(2,1)}), bf16[16,1,128,640]{3,2,1,0:T(8,128)(2,1)S(1)}, u32[]{:S(2)}, u32[]{:S(2)}) %all-to-all-start.4) | async-done | bytes 2621472 | tf_op jit(solution)/shard_map/all_to_all | solution.py:141
  897.5 1.5 gather_fusion.8
  899.0 2.1 broadcast_select_fusion
  (342 shorter events, 64.5 us)
Async XLA Ops:
  7.2 2.0 copy-start
  9.1 2.4 copy-start.2
  11.5 2.4 copy-start.3
  13.9 2.4 copy-start.4
  157.0 3.9 copy-start.8
  157.0 64.7 %all-to-all-start.2 = ((bf16[16,1,128,640]{3,2,1,0:T(8,128)(2,1)}), bf16[16,1,128,640]{3,2,1,0:T(8,128)(2,1)S(1)}, u32[]{:S(2)}, u32[]{:S(2)}) async-start(bf16[16,1,128,640]{3,2,1,0:T(8,128)(2,1)} %get-tuple-element.148), calls=%async_computation.2 | async-start | bytes 5242880 | tf_op jit(solution)/shard_map/all_to_all | solution.py:72
  231.0 6.2 copy-start.5
  231.0 292.1 %all-to-all-start.3 = ((bf16[16,512,640]{1,2,0:T(8,128)(2,1)}), bf16[16,512,640]{1,2,0:T(8,128)(2,1)}, u32[]{:S(2)}, u32[]{:S(2)}) async-start(bf16[16,512,640]{1,2,0:T(8,128)(2,1)} %stack.3), calls=%async_computation.3 | async-start | bytes 20971520 | tf_op jit(solution)/shard_map/all_to_all | solution.py:119
  236.0 388.1 %all-gather.2.cloned.1.call-start = ((), (), s32[]{:S(2)}) async-start(), calls=%async_computation.5 | async-start | bytes 11141120 | tf_op jit(solution)/shard_map/all_gather | solution.py:117
  625.8 4.8 copy-start.6
  629.3 5.9 slice-start
  630.6 4.6 slice-start.1
  635.1 1.3 copy-start.7
  638.1 4.8 copy-start.6
  641.6 5.8 slice-start
  643.0 4.5 slice-start.1
  647.5 1.3 copy-start.7
  650.5 4.8 copy-start.6
  654.0 5.8 slice-start
  655.3 4.5 slice-start.1
  662.9 4.8 copy-start.6
  666.4 5.8 slice-start
  667.7 4.5 slice-start.1
  672.3 1.3 copy-start.7
  675.3 4.8 copy-start.6
  678.8 5.8 slice-start
  680.1 4.5 slice-start.1
  684.7 1.3 copy-start.7
  687.7 4.8 copy-start.6
  691.2 5.8 slice-start
  692.5 4.5 slice-start.1
  700.0 4.8 copy-start.6
  703.5 5.8 slice-start
  704.8 4.5 slice-start.1
  709.4 1.3 copy-start.7
  712.4 4.8 copy-start.6
  715.9 5.8 slice-start
  717.2 4.5 slice-start.1
  724.8 4.8 copy-start.6
  728.3 5.8 slice-start
  729.6 4.5 slice-start.1
  737.2 4.8 copy-start.6
  740.7 5.8 slice-start
  742.0 4.5 slice-start.1
  749.5 4.8 copy-start.6
  753.1 5.8 slice-start
  754.4 4.5 slice-start.1
  761.9 4.8 copy-start.6
  765.4 5.8 slice-start
  766.7 4.5 slice-start.1
  774.3 4.8 copy-start.6
  777.8 5.8 slice-start
  779.1 4.5 slice-start.1
  786.7 4.8 copy-start.6
  790.2 5.8 slice-start
  791.5 4.5 slice-start.1
  799.1 4.8 copy-start.6
  802.6 5.8 slice-start
  803.9 4.5 slice-start.1
  811.4 4.8 copy-start.6
  814.9 5.8 slice-start
  816.3 4.5 slice-start.1
  827.7 69.8 %all-to-all-start.4 = ((bf16[16,1,128,640]{3,2,1,0:T(8,128)(2,1)}), bf16[16,1,128,640]{3,2,1,0:T(8,128)(2,1)S(1)}, u32[]{:S(2)}, u32[]{:S(2)}) async-start(bf16[16,1,128,640]{3,2,1,0:T(8,128)(2,1)} %fusion.17), calls=%async_computation.4 | async-start | bytes 5242880 | tf_op jit(solution)/shard_map/all_to_all | solution.py:141
  836.8 64.2 %copy-start.1 = (bf16[512,640]{1,0:T(8,128)(2,1)S(1)}, bf16[512,640]{1,0:T(8,128)(2,1)}, u32[]{:S(2)}) copy-start(bf16[512,640]{1,0:T(8,128)(2,1)} %param.11) | copy-start | bytes 1966084
  (11 other events, 14.2 us)
Sparse Core Ops, SparseCore 0:
  239.2 384.9 all-gather.1
